TPU v7x, 32 devices: a whole 2x2x4 slice. The times are simulated.
32 devices in a mesh: ep: 8 (over z, x), rep: 4 (over y, core).
Axes of the slice: x: 2, y: 2, z: 4, core: 2. Of those that a mesh axis runs over, the one named last changes fastest.
Arguments:
- quant_in: bfloat16 [8, 7168, 2048], P('ep', 'rep'), may hold values from -1 to 1
- scale_in: float32 [8, 56, 16], P('ep', 'rep'), may hold values from 0.002 to 0.02
- b_train: bfloat16 [8, 7168, 64], P('ep', None, 'rep'), may hold values from -0.041992188 to 0.041992188
- a_train: bfloat16 [8, 64, 2048], P('ep', 'rep'), may hold values from -0.59765625 to 0.59765625
- adapter_ranks: int32 [8], replicated, may hold values from 0 to 64
- trainer_map: int32 [8], replicated, may hold values from 0 to 7, each once
- hot_plan: int32 [4], replicated, may hold values from 0 to 7, as said below
Outputs:
- quant_out: bfloat16 [8, 7168, 2048], P('ep', 'rep')
- scale_out: float32 [8, 56, 16], P('ep', 'rep')
- hot_values: bfloat16 [4, 7168, 2048], P(None, ('rep', 'ep'))
- replica_block_scales: float32 [4, 56, 16], P(None, 'rep')
Inputs may be any that keep to these rules, and one draw needn't show every extreme that they name: `hot_plan`: 4 distinct expert numbers.
All inputs are finite; a program needn't handle non-finite values. Where the computation divides by a largest or mean magnitude, that divisor is 1e-20 or more.
Results may differ from a plain program's by a relative error of at most 0.001.
Values may be sent and summed in bfloat16 or wider, within the bound.
A program may use at most 128 MiB of HBM per device.

v0:
```python
import jax
import jax.numpy as jnp
from jax import lax
from jax.sharding import PartitionSpec as P

BLOCK = 128
RMAX = 64


EPS = 1e-06


def body(quant_in, scale_in, b_train, a_train, adapter_ranks, trainer_map, hot_plan):
    exp_dev = quant_in.shape[0]
    rows = quant_in.shape[1]
    cols = quant_in.shape[2]
    owner = lax.axis_index("ep")
    owned_expert_index = owner * exp_dev + jnp.arange(exp_dev, dtype=jnp.int32)
    b_rows = lax.all_to_all(b_train, "rep", split_axis=1, concat_axis=2, tiled=True)
    a_full = lax.all_gather(a_train, "rep", axis=1, tiled=True)
    rank_selector = (trainer_map[None, :] == owned_expert_index[:, None]).astype(jnp.bfloat16)
    b_sum = jnp.einsum(
        "ji,idr->jdr",
        rank_selector,
        lax.all_gather(b_rows, "ep", axis=0, tiled=True),
        preferred_element_type=jnp.float32,
    )
    a_sum = jnp.einsum(
        "ji,irf->jrf",
        rank_selector,
        lax.all_gather(a_full, "ep", axis=0, tiled=True),
        preferred_element_type=jnp.float32,
    )
    serving_up_factor = b_sum.astype(jnp.bfloat16)
    a_serv = a_sum.astype(jnp.bfloat16)
    local_rank_indices = lax.dynamic_slice_in_dim(adapter_ranks, owner * exp_dev, exp_dev, 0)
    live = (jnp.arange(RMAX, dtype=jnp.int32)[None, :] < local_rank_indices[:, None]).astype(
        jnp.bfloat16
    )
    active_down_factor = a_serv * live[:, :, None]
    weight_update = jnp.einsum(
        "enw,ewk->enk", serving_up_factor, active_down_factor, preferred_element_type=jnp.float32
    )
    row_blocks = rows // BLOCK
    col_blocks = cols // BLOCK
    expert_weight_tensor = (
        quant_in.astype(jnp.float32).reshape(exp_dev, row_blocks, BLOCK, col_blocks, BLOCK)
        * scale_in[:, :, None, :, None]
    )
    merged = expert_weight_tensor + weight_update.reshape(
        exp_dev, row_blocks, BLOCK, col_blocks, BLOCK
    )
    scale_out = jnp.max(jnp.abs(merged), axis=(2, 4)) + EPS
    quant_out = (
        (merged / scale_out[:, :, None, :, None]).reshape(exp_dev, rows, cols).astype(jnp.bfloat16)
    )
    received = lax.all_to_all(quant_out, "ep", split_axis=1, concat_axis=0, tiled=True)
    total = received.shape[0]
    rank_selector = (hot_plan[:, None] == jnp.arange(total, dtype=jnp.int32)[None, :]).astype(
        jnp.bfloat16
    )
    hot_values = jnp.einsum(
        "je,edf->jdf", rank_selector, received, preferred_element_type=jnp.float32
    ).astype(jnp.bfloat16)
    all_scales = lax.all_gather(scale_out, "ep", axis=0, tiled=True)
    every = all_scales.shape[0]
    scale_select = (hot_plan[:, None] == jnp.arange(every, dtype=jnp.int32)[None, :]).astype(
        jnp.float32
    )
    replica_block_scales = jnp.einsum(
        "je,ebc->jbc", scale_select, all_scales, precision=lax.Precision.HIGHEST
    )
    return (quant_out, scale_out, hot_values, replica_block_scales)


def solution(mesh):
    placed = (
        P("ep", "rep", None),
        P("ep", "rep", None),
        P("ep", None, "rep"),
        P("ep", "rep", None),
        P(),
        P(),
        P(),
    )
    return jax.shard_map(
        body,
        mesh=mesh,
        in_specs=placed,
        out_specs=(
            P("ep", "rep", None),
            P("ep", "rep", None),
            P(None, ("rep", "ep"), None),
            P(None, "rep", None),
        ),
        check_vma=False,
    )
```

profile of v0, /device:TPU:0, one launch (start us, length us, event | category | flops | bytes accessed | tf_op | source)
XLA Modules:
  0.0 523.5 jit_solution(16869840102661189004)
XLA Ops:
  7.2 0.0 all-gather.5.cloned.1.call-start
  7.2 7.6 %copy.26 = bf16[1,7168,16]{2,0,1:T(2,128)(2,1)} copy(bf16[1,7168,16]{1,2,0:T(8,128)(2,1)} %param.9) | data formatting | bytes 458752 | tf_op args[2]
  14.8 0.5 broadcast.33
  15.3 0.0 copy-start
  15.3 39.8 %reduce.2 = bf16[7168,16]{1,0:T(8,128)(2,1)S(1)} reduce(bf16[7168,1,16]{2,1,0:T(2,128)(2,1)} %bitcast.67, bf16[]{:T(256)} %broadcast.33), dimensions={1}, to_apply=%bitcast.48.reduce_sub_computation | reduce | bytes 458754
  55.1 0.0 copy-start.1
  55.2 1.9 reshape.111
  57.1 9.7 %all_to_all.30 = bf16[4,2,14336]{2,1,0:T(2,128)(2,1)S(1)} all-to-all(bf16[4,2,14336]{2,1,0:T(2,128)(2,1)S(1)} %reshape.111), channel_id=1, replica_groups=mesh['ep'=8,'rep'=4] {'rep'}, dimensions={0} | all-to-all | bytes 458752 | tf_op jit(solution)/shard_map/all_to_all | solution.py:19
  66.8 3.6 reshape.112
  70.4 6.9 %copy.27 = bf16[1,7168,16]{1,2,0:T(8,128)(2,1)S(1)} copy(bf16[1,7168,16]{2,0,1:T(2,128)(2,1)} %bitcast.68) | data formatting | bytes 458752 | tf_op jit(solution)/shard_map/all_to_all | solution.py:19
  77.3 0.2 all_to_all.23
  77.5 0.7 copy.28
  78.2 0.0 all-gather.5.cloned.1.call-update
  78.2 0.0 all-gather.7.cloned.1.call-start
  78.3 0.0 copy-done
  78.3 6.4 %all_gather.13 = bf16[1,64,2048]{2,1,0:T(8,128)(2,1)} all-gather(bf16[1,16,2048]{2,1,0:T(8,128)(2,1)S(1)} %copy-done), channel_id=1, replica_groups=mesh['ep'=8,'rep'=4] {'rep'}, dimensions={1}, use_global_device_ids=true | all-gather | bytes 327680 | tf_op jit(solution)/shard_map/all_gather | solution.py:20
  84.7 0.0 all-gather.7.cloned.1.call-update
  84.7 0.0 copy-done.1
  84.7 10.3 %convert_bitcast_fusion = f32[224,8,16,128]{3,1,2,0:T(8,128)} fusion(bf16[1,1792,2048]{2,1,0:T(8,128)(2,1)} %param.7), kind=kLoop, calls=%fused_computation.2 | loop fusion | flops 3670016 | bytes 22020096
  95.1 0.0 copy-start.4
  95.1 14.1 %copy.47 = f32[224,8,16,128]{3,2,1,0:T(8,128)} copy(f32[224,8,16,128]{3,1,2,0:T(8,128)} %convert_bitcast_fusion) | data formatting | bytes 29360128
  109.2 0.0 copy-done.4
  109.2 0.6 dynamic_slice.3
  109.7 0.6 compare_convert_fusion
  110.4 14.7 %all-gather.5.cloned.1.call-done = bf16[8,1792,64]{1,2,0:T(8,128)(2,1)} async-done(((bf16[1,1792,64]{1,2,0:T(8,128)(2,1)}), bf16[8,1792,64]{1,2,0:T(8,128)(2,1)}) %all-gather.5.cloned.1.call-update) | async-done | bytes 1835024 | tf_op jit(solution)/shard_map/all_gather | solution.py:25
  125.1 0.0 copy-done.2
  125.1 18.2 %fusion.8 = bf16[1,1792,64]{0,1,2:T(8,128)(2,1)} fusion(bf16[8,1792,64]{1,2,0:T(8,128)(2,1)} %all-gather.5.cloned.1.call-done, s32[8]{0:T(128)S(1)} %copy-done.2, s32[]{:T(128)S(6)} %axis_index.15), kind=kOutput, calls=%fused_computation.10 | convolution fusion | flops 1835016 | bytes 2064420 | tf_op jit(solution)/shard_map/ji,idr->jdr/dot_general | solution.py:22
  143.2 22.6 %copy.38 = bf16[1,1792,64]{1,2,0:T(8,128)(2,1)S(1)} copy(bf16[1,1792,64]{0,1,2:T(8,128)(2,1)} %fusion.8) | data formatting | bytes 458752 | tf_op jit(solution)/shard_map/ji,idr->jdr/dot_general | solution.py:22
  165.9 0.2 dot_general.20
  166.1 9.0 %all-gather.7.cloned.1.call-done = bf16[8,64,2048]{2,1,0:T(8,128)(2,1)} async-done(((bf16[1,64,2048]{2,1,0:T(8,128)(2,1)}), bf16[8,64,2048]{2,1,0:T(8,128)(2,1)}) %all-gather.7.cloned.1.call-update) | async-done | bytes 2097168 | tf_op jit(solution)/shard_map/all_gather | solution.py:31
  175.0 3.2 fusion.6
  178.2 13.3 %abs_reduce_fusion = (f32[14,16]{1,0:T(8,128)S(1)}, f32[14,128,16,128]{3,1,2,0:T(8,128)}) fusion(bf16[14,128,64,1]{1,0,2,3:T(8,128)(2,1)S(1)} %bitcast.69, f32[14,16]{1,0:T(8,128)S(1)} %bitcast.73, f32[14,128,16,128]{3,2,1,0:T(8,128)} %bitcast.63, bf16[1,64,2048]{2,0,1:T(2,128)(2,1)S(1)} %fusion.6, bf16[64]{0:T(256)(128)(2,1)S(1)} %compare_convert_fusion), kind=kOutput, calls=%fused_computation.4 | convolution fusion | flops 484572960 | bytes 29853568 | tf_op jit(solution)/shard_map/enw,ewk->enk/dot_general | solution.py:41
  191.5 10.4 %divide_convert_fusion = bf16[14,128,16,128]{3,1,2,0:T(8,128)(2,1)} fusion(f32[14,128,16,128]{3,1,2,0:T(8,128)} %get-tuple-element.23, f32[14,16]{1,0:T(8,128)S(1)} %get-tuple-element.21), kind=kLoop, calls=%fused_computation.3 | loop fusion | flops 7340032 | bytes 22020992 | tf_op jit(solution)/shard_map/convert_element_type | solution.py:55
  201.9 12.0 %copy.31 = bf16[14,128,16,128]{3,2,1,0:T(8,128)(2,1)} copy(bf16[14,128,16,128]{3,1,2,0:T(8,128)(2,1)} %divide_convert_fusion) | data formatting | bytes 14680064 | tf_op jit(solution)/shard_map/convert_element_type | solution.py:55
  213.9 11.8 %convert_element_type.44 = bf16[1,1792,2048]{2,1,0:T(8,128)(2,1)} reshape(bf16[14,128,16,128]{3,2,1,0:T(8,128)(2,1)} %copy.31) | data formatting | bytes 14680064 | tf_op jit(solution)/shard_map/convert_element_type | solution.py:55
  225.7 13.7 %copy.81 = bf16[1,1792,2048]{2,0,1:T(2,128)(2,1)} copy(bf16[1,1792,2048]{2,1,0:T(8,128)(2,1)} %convert_element_type.44) | data formatting | bytes 14680064 | tf_op jit(solution)/shard_map/convert_element_type | solution.py:55
  239.4 45.0 %reduce.3 = bf16[1792,2048]{1,0:T(8,128)(2,1)} reduce(bf16[1792,1,2048]{2,1,0:T(2,128)(2,1)} %bitcast.64, bf16[]{:T(256)} %broadcast.33), dimensions={1}, to_apply=%bitcast.62.reduce_sub_computation | reduce | bytes 14680066
  284.4 10.2 %reshape.113 = bf16[8,2,229376]{2,1,0:T(2,128)(2,1)} reshape(bf16[1792,2048]{1,0:T(8,128)(2,1)} %reduce.3) | data formatting | bytes 14680064
  294.6 5.0 all-to-all-start.1
  299.6 0.6 copy.35
  300.2 178.3 %all-gather.1 = f32[8,14,16]{2,1,0:T(8,128)S(1)} all-gather(f32[1,14,16]{2,1,0:T(8,128)S(1)} %get-tuple-element.20), channel_id=2, replica_groups=mesh['ep'=8,'rep'=4] {'ep'}, dimensions={0}, use_global_device_ids=true | all-gather | bytes 8064 | tf_op jit(solution)/shard_map/all_gather | solution.py:65
  478.5 0.0 copy-done.3
  478.5 0.8 fusion.14
  479.3 0.0 all-to-all-done.1
  479.3 12.3 %reshape.114 = bf16[1792,1,2048]{2,1,0:T(2,128)(2,1)} reshape(bf16[8,2,229376]{2,1,0:T(2,128)(2,1)} %all-to-all-done.1) | data formatting | bytes 14680064
  491.6 12.8 %copy.45 = bf16[1,1792,2048]{2,1,0:T(8,128)(2,1)} copy(bf16[1,1792,2048]{2,0,1:T(2,128)(2,1)} %bitcast.65) | data formatting | bytes 14680064
  504.4 8.2 %fusion.3 = bf16[4,224,2048]{2,0,1:T(4,128)(2,1)S(1)} fusion(bf16[8,224,2048]{2,1,0:T(8,128)(2,1)} %bitcast.66, s32[4]{0:T(128)S(1)} %copy-done.3), kind=kOutput, calls=%fused_computation.7 | convolution fusion | flops 31195168 | bytes 11010064 | tf_op jit(solution)/shard_map/je,edf->jdf/dot_general | solution.py:62
  512.6 3.8 copy.36
  (4 shorter events, 0.0 us)
Async XLA Ops:
  7.2 117.9 %all-gather.5.cloned.1.call-start = ((), (), s32[]{:S(2)}) async-start(), calls=%async_computation.2 | async-start | bytes 2064384 | tf_op jit(solution)/shard_map/all_gather | solution.py:25
  15.3 63.0 %copy-start = (bf16[1,16,2048]{2,1,0:T(8,128)(2,1)S(1)}, bf16[1,16,2048]{2,1,0:T(8,128)(2,1)}, u32[]{:S(2)}) copy-start(bf16[1,16,2048]{2,1,0:T(8,128)(2,1)} %param.10) | copy-start | bytes 196612
  55.1 29.6 %copy-start.1 = (f32[1,14,16]{2,0,1:T(1,128)S(1)}, f32[1,14,16]{2,0,1:T(1,128)}, u32[]{:S(2)}) copy-start(f32[1,14,16]{2,0,1:T(1,128)} %param.8) | copy-start | bytes 2692
  78.2 96.8 %all-gather.7.cloned.1.call-start = ((), (), s32[]{:S(2)}) async-start(), calls=%async_computation.3 | async-start | bytes 2359296 | tf_op jit(solution)/shard_map/all_gather | solution.py:31
  95.1 14.1 %copy-start.4 = (s32[8]{0:T(128)S(1)}, s32[8]{0:T(128)}, u32[]{:S(2)}) copy-start(s32[8]{0:T(128)} %param.11) | copy-start | bytes 100
  95.1 30.0 %copy-start.2 = (s32[8]{0:T(128)S(1)}, s32[8]{0:T(128)}, u32[]{:S(2)}) copy-start(s32[8]{0:T(128)} %param.12) | copy-start | bytes 100
  294.6 183.9 %copy-start.3 = (s32[4]{0:T(128)S(1)}, s32[4]{0:T(128)}, u32[]{:S(2)}) copy-start(s32[4]{0:T(128)} %param.13) | copy-start | bytes 52
  294.6 184.7 %all-to-all-start.1 = ((bf16[8,2,229376]{2,1,0:T(2,128)(2,1)}), bf16[8,2,229376]{2,1,0:T(2,128)(2,1)}, u32[]{:S(2)}, u32[]{:S(2)}) async-start(bf16[8,2,229376]{2,1,0:T(2,128)(2,1)} %reshape.113), calls=%async_computation.1 | async-start | bytes 14680064 | tf_op jit(solution)/shard_map/all_to_all | solution.py:57
Sparse Core Ops, SparseCore 0:
  78.4 46.6 all-gather.4
  127.2 47.7 all-gather.6
where the time goes:
time: 532 us; the launch traced here: 524 us
  blocking collectives  194 us (36%)
  local copies, waits for them, and re-layouts  136 us (26%)
  other arithmetic  106 us (20%)
  matrix products  43.6 us (8%)
  waiting for transfers between devices  23.7 us (4%)
  between operations  14.4 us (3%)
    all_gather x1, blocking collectives, body(): all_scales = lax.all_gather(scale_out, 'ep', axis=0, tiled=True)  178 us
    unnamed x3, other arithmetic  95.1 us
    unnamed x21, local copies, waits for them, and re-layouts  67.5 us
    convert_element_type x3, local copies, waits for them, and re-layouts, body(): (merged / scale_out[:, :, None, :, None]).reshape(exp_dev, rows, cols)  37.5 us
    dot_general x1, local copies, waits for them, and re-layouts, body(): jnp.einsum('ji,idr->jdr', rank_selector, lax.all_gather(b_rows, 'ep', axi...  22.6 us
    dot_general x1, matrix products, body(): jnp.einsum('ji,idr->jdr', rank_selector, lax.all_gather(b_rows, 'ep', axi...  18.2 us
    all_gather x1, waiting for transfers between devices, body(): lax.all_gather(b_rows, 'ep', axis=0, tiled=True)  14.7 us
    dot_general x1, matrix products, body(): jnp.einsum('enw,ewk->enk', serving_up_factor, active_down_factor, preferr...  13.3 us
  transfers between devices with their start and end apart: 3, of which 2 were waited for; matrix products, arithmetic and copies ran while one was open for 13% of the time, Pallas kernels for 0%

commit v1 on v0

--- a/solution.py
+++ b/solution.py
@@ -1,6 +1,12 @@
+import functools
+import itertools
+import math
+
 import jax
 import jax.numpy as jnp
 from jax import lax
+from jax.experimental import pallas as pl
+from jax.experimental.pallas import tpu as pltpu
 from jax.sharding import PartitionSpec as P
 
 BLOCK = 128
@@ -8,6 +14,350 @@
 
 
 EPS = 1e-06
+MAX_PLANS = 0
+MESH = pl.DeviceIdType.MESH
+
+
+def exchange_kernel(n, reps, pieces, wide, cols, inv, b_ref, a_ref, bt_out, a_out,
+                    b_mid, a_mid, b_stage, a_stage,
+                    sb1, rb1, sa1, ra1, sb2, rb2, sa2, ra2):
+    ep = lax.axis_index("ep")
+    rep = lax.axis_index("rep")
+    slab = pieces * wide
+    barrier = pltpu.get_barrier_semaphore()
+    for de in range(n):
+        for dr in range(reps):
+            if de or dr:
+                pl.semaphore_signal(
+                    barrier,
+                    inc=1,
+                    device_id={"ep": lax.rem(ep + de, n), "rep": lax.rem(rep + dr, reps)},
+                    device_id_type=MESH,
+                )
+    pl.semaphore_wait(barrier, n * reps - 1)
+
+    def move(own, src, dst, send, recv, de, dr):
+        if own:
+            return pltpu.make_async_copy(src, dst, recv)
+        return pltpu.make_async_remote_copy(
+            src_ref=src,
+            dst_ref=dst,
+            send_sem=send,
+            recv_sem=recv,
+            device_id={"ep": lax.rem(ep + de, n), "rep": lax.rem(rep + dr, reps)},
+            device_id_type=MESH,
+        )
+
+    def b_first(de, dr):
+        j, q = lax.rem(ep + de, n), lax.rem(rep + dr, reps)
+        at = q * slab + jnp.minimum(j, pieces - 1) * wide
+        src = b_ref.at[0, :, pl.ds(pl.multiple_of(at, BLOCK), wide)]
+        return j, move(not (de or dr), src, b_mid.at[ep, rep], sb1.at[de, dr], rb1.at[ep, rep], de, dr)
+
+    def a_first(de):
+        j = lax.rem(ep + de, n)
+        src = a_ref.at[0, :, pl.ds(pl.multiple_of(j * cols, cols), cols)]
+        return move(de == 0, src, a_mid.at[ep], sa1.at[de], ra1.at[ep], de, 0)
+
+    order = [(de, dr) for de in reversed(range(n)) for dr in range(reps)]
+    for de in reversed(range(n)):
+        a_first(de).start()
+    for de, dr in order:
+        j, copy = b_first(de, dr)
+        pl.when(j < pieces)(copy.start)
+
+    for s in range(n):
+        pltpu.make_async_copy(a_mid.at[s], a_mid.at[s], ra1.at[s]).wait()
+    for d in range(n):
+        a_stage[d] = a_mid[inv[d]]
+
+    def a_second(de, dr):
+        d = lax.rem(ep + de, n)
+        dst = a_out.at[rep, :, pl.ds(pl.multiple_of(ep * cols, cols), cols)]
+        return move(not (de or dr), a_stage.at[d], dst, sa2.at[de, dr], ra2.at[ep, rep], de, dr)
+
+    def b_second(de):
+        d = lax.rem(ep + de, n)
+        here = jnp.minimum(ep, pieces - 1)
+        dst = bt_out.at[:, :, pl.ds(pl.multiple_of(here * wide, wide), wide)]
+        return move(de == 0, b_stage.at[d], dst, sb2.at[de], rb2.at[ep], de, 0)
+
+    for de, dr in order:
+        a_second(de, dr).start()
+
+    @pl.when(ep < pieces)
+    def _():
+        for s in range(n):
+            for r in range(reps):
+                pltpu.make_async_copy(b_mid.at[s, r], b_mid.at[s, r], rb1.at[s, r]).wait()
+        for d in range(n):
+            b_stage[d] = b_mid[inv[d]]
+        for de in reversed(range(n)):
+            b_second(de).start()
+
+    for j in range(n):
+        for q in range(reps):
+            dst = a_out.at[q, :, pl.ds(j * cols, cols)]
+            pltpu.make_async_copy(dst, dst, ra2.at[j, q]).wait()
+    for j in range(pieces):
+        dst = bt_out.at[:, :, pl.ds(j * wide, wide)]
+        pltpu.make_async_copy(dst, dst, rb2.at[j]).wait()
+    for de, dr in order:
+        if de or dr:
+            j, copy = b_first(de, dr)
+            pl.when(j < pieces)(copy.wait_send)
+            a_second(de, dr).wait_send()
+    for de in range(1, n):
+        a_first(de).wait_send()
+        copy = b_second(de)
+        pl.when(ep < pieces)(copy.wait_send)
+
+
+def exchange(inv, b_train, a_train, n, reps):
+    depth, ranks = b_train.shape[1:]
+    features = a_train.shape[2]
+    slab = depth // reps
+    blocks = slab // BLOCK
+    wide = -(-blocks // n) * BLOCK
+    pieces = slab // wide
+    cols = features // n
+    bf16 = jnp.bfloat16
+    dma = pltpu.SemaphoreType.DMA
+    return pl.pallas_call(
+        functools.partial(exchange_kernel, n, reps, pieces, wide, cols),
+        out_shape=(
+            jax.ShapeDtypeStruct((reps, ranks, slab), bf16),
+            jax.ShapeDtypeStruct((reps, ranks, features), bf16),
+        ),
+        in_specs=[
+            pl.BlockSpec(memory_space=pltpu.SMEM),
+            pl.BlockSpec(memory_space=pltpu.VMEM),
+            pl.BlockSpec(memory_space=pltpu.VMEM),
+        ],
+        out_specs=(pl.BlockSpec(memory_space=pltpu.VMEM),) * 2,
+        scratch_shapes=[
+            pltpu.VMEM((n, reps, ranks, wide), bf16),
+            pltpu.VMEM((n, ranks, cols), bf16),
+            pltpu.VMEM((n, reps, ranks, wide), bf16),
+            pltpu.VMEM((n, ranks, cols), bf16),
+            dma((n, reps)), dma((n, reps)), dma((n,)), dma((n,)),
+            dma((n,)), dma((n,)), dma((n, reps)), dma((n, reps)),
+        ],
+        compiler_params=pltpu.CompilerParams(
+            collective_id=0, has_side_effects=True, vmem_limit_bytes=32 << 20
+        ),
+        name="exchange",
+    )(inv, jnp.swapaxes(b_train, 1, 2), a_train)
+
+
+def merge_kernel(rank, scale_in, quant_in, bt, a, quant_out, scale_out, live):
+    step = pl.program_id(0)
+    blocks = quant_in.shape[1] // BLOCK
+    col_blocks = quant_in.shape[2] // BLOCK
+
+    @pl.when(step == 0)
+    def _():
+        keep = lax.broadcasted_iota(jnp.int32, live.shape, 0) < rank[0]
+        live[...] = jnp.where(keep, a[...].astype(jnp.float32), 0.0).astype(jnp.bfloat16)
+
+    lane = lax.broadcasted_iota(jnp.int32, (1, col_blocks), 1)
+    for i in range(blocks):
+        delta = lax.dot_general(
+            bt[:, i * BLOCK:(i + 1) * BLOCK], live[...], (((0,), (0,)), ((), ())),
+            preferred_element_type=jnp.float32,
+        )
+        rows = slice(i * BLOCK, (i + 1) * BLOCK)
+        found = jnp.zeros((1, col_blocks), jnp.float32)
+        for c in range(col_blocks):
+            cut = slice(c * BLOCK, (c + 1) * BLOCK)
+            held = quant_in[0, rows, cut].astype(jnp.float32)
+            merged = held * scale_in[0, step * blocks + i, c] + delta[:, cut]
+            top = jnp.max(jnp.max(jnp.abs(merged), axis=0, keepdims=True), axis=1, keepdims=True) + EPS
+            quant_out[0, rows, cut] = (merged * (1.0 / top)).astype(jnp.bfloat16)
+            found = jnp.where(lane == c, top, found)
+        scale_out[0, pl.ds(step * blocks + i, 1), :] = found
+
+
+def merge(rank, scale_in, quant_in, bt, a):
+    _, rows, features = quant_in.shape
+    total = rows // BLOCK
+    blocks = 2 if total % 2 == 0 else 1
+    steps = total // blocks
+    tall = blocks * BLOCK
+    return pl.pallas_call(
+        merge_kernel,
+        grid=(steps,),
+        out_shape=(
+            jax.ShapeDtypeStruct(quant_in.shape, jnp.bfloat16),
+            jax.ShapeDtypeStruct(scale_in.shape, jnp.float32),
+        ),
+        in_specs=[
+            pl.BlockSpec(memory_space=pltpu.SMEM),
+            pl.BlockSpec(memory_space=pltpu.SMEM),
+            pl.BlockSpec((1, tall, features), lambda i: (0, i, 0)),
+            pl.BlockSpec((bt.shape[0], tall), lambda i: (0, i)),
+            pl.BlockSpec(a.shape, lambda i: (0, 0)),
+        ],
+        out_specs=(
+            pl.BlockSpec((1, tall, features), lambda i: (0, i, 0)),
+            pl.BlockSpec(scale_in.shape, lambda i: (0, 0, 0)),
+        ),
+        scratch_shapes=[pltpu.VMEM(a.shape, jnp.bfloat16)],
+        compiler_params=pltpu.CompilerParams(vmem_limit_bytes=32 << 20),
+        name="merge",
+    )(rank, scale_in, quant_in, bt, a)
+
+
+def hot_kernel(n, sources, piece, quant, scale, slots, scales, send, recv, ssend, srecv):
+    ep = lax.axis_index("ep")
+    barrier = pltpu.get_barrier_semaphore()
+    for de in range(1, n):
+        pl.semaphore_signal(
+            barrier, inc=1, device_id={"ep": lax.rem(ep + de, n)}, device_id_type=MESH
+        )
+    pl.semaphore_wait(barrier, n - 1)
+
+    def scale_copy(de):
+        return pltpu.make_async_remote_copy(
+            src_ref=scale, dst_ref=scales.at[pl.ds(ep, 1)], send_sem=ssend.at[de],
+            recv_sem=srecv.at[ep], device_id={"ep": lax.rem(ep + de, n)}, device_id_type=MESH,
+        )
+
+    def piece_copy(k, p):
+        return pltpu.make_async_remote_copy(
+            src_ref=quant.at[0, pl.ds(p * piece, piece)], dst_ref=slots.at[k],
+            send_sem=send.at[p], recv_sem=recv.at[k], device_id={"ep": p}, device_id_type=MESH,
+        )
+
+    def own_copy(k, p):
+        return pltpu.make_async_copy(quant.at[0, pl.ds(p * piece, piece)], slots.at[k], recv.at[k])
+
+    own_scale = pltpu.make_async_copy(scale, scales.at[pl.ds(ep, 1)], srecv.at[ep])
+    own_scale.start()
+    for de in range(1, n):
+        scale_copy(de).start()
+    for k, e in enumerate(sources):
+        @pl.when(ep == e)
+        def _():
+            for p in range(n):
+                if p != e:
+                    piece_copy(k, p).start()
+            own_copy(k, e).start()
+    for k in range(len(sources)):
+        pltpu.make_async_copy(slots.at[k], slots.at[k], recv.at[k]).wait()
+    for k, e in enumerate(sources):
+        @pl.when(ep == e)
+        def _():
+            for p in range(n):
+                if p != e:
+                    piece_copy(k, p).wait_send()
+    for s in range(n):
+        pltpu.make_async_copy(scales.at[pl.ds(s, 1)], scales.at[pl.ds(s, 1)], srecv.at[s]).wait()
+    for de in range(1, n):
+        scale_copy(de).wait_send()
+
+
+def spread(quant, scale, n, sources, collective_id):
+    piece = quant.shape[1] // n
+    dma = pltpu.SemaphoreType.DMA
+    return pl.pallas_call(
+        functools.partial(hot_kernel, n, sources, piece),
+        out_shape=(
+            jax.ShapeDtypeStruct((len(sources), piece, quant.shape[2]), quant.dtype),
+            jax.ShapeDtypeStruct((n,) + scale.shape[1:], scale.dtype),
+        ),
+        in_specs=[
+            pl.BlockSpec(memory_space=pl.ANY),
+            pl.BlockSpec(memory_space=pltpu.VMEM),
+        ],
+        out_specs=(
+            pl.BlockSpec(memory_space=pl.ANY),
+            pl.BlockSpec(memory_space=pltpu.VMEM),
+        ),
+        scratch_shapes=[dma((n,)), dma((len(sources),)), dma((n,)), dma((n,))],
+        compiler_params=pltpu.CompilerParams(collective_id=collective_id, has_side_effects=True),
+        name="spread",
+    )(quant, scale)
+
+
+def place_kernel(where, plan, held, scales, values, picked):
+    values[...] = held[...]
+
+    @pl.when(pl.program_id(0) == 0)
+    def _():
+        for k in range(picked.shape[0]):
+            picked[k] = scales[plan[k]]
+
+
+def place(where, plan, slots, scales):
+    count = plan.shape[0]
+    block = (1,) + slots.shape[1:]
+    return pl.pallas_call(
+        place_kernel,
+        grid_spec=pltpu.PrefetchScalarGridSpec(
+            num_scalar_prefetch=2,
+            grid=(count,),
+            in_specs=[
+                pl.BlockSpec(block, lambda k, where, plan: (where[k], 0, 0)),
+                pl.BlockSpec(scales.shape, lambda k, where, plan: (0, 0, 0)),
+            ],
+            out_specs=[
+                pl.BlockSpec(block, lambda k, where, plan: (k, 0, 0)),
+                pl.BlockSpec((count,) + scales.shape[1:], lambda k, where, plan: (0, 0, 0)),
+            ],
+        ),
+        out_shape=(
+            jax.ShapeDtypeStruct((count,) + slots.shape[1:], slots.dtype),
+            jax.ShapeDtypeStruct((count,) + scales.shape[1:], scales.dtype),
+        ),
+        compiler_params=pltpu.CompilerParams(vmem_limit_bytes=32 << 20),
+        name="place",
+    )(where, plan, slots, scales)
+
+
+def kernel_body(n, reps, quant_in, scale_in, b_train, a_train, adapter_ranks, trainer_map, hot_plan):
+    owner = lax.axis_index("ep")
+    serving = jnp.arange(n, dtype=jnp.int32)
+    inv = jnp.sum(
+        jnp.where(trainer_map[None, :] == serving[:, None], serving[None, :], 0), axis=1
+    ).astype(jnp.int32)
+    bt, a = exchange(inv, b_train, a_train, n, reps)
+    bt = bt.reshape(-1, bt.shape[2])
+    a = a.reshape(-1, a.shape[2])
+    rank = lax.dynamic_slice_in_dim(adapter_ranks, owner, 1, 0)
+    quant_out, scale_out = merge(rank, scale_in, quant_in, bt, a)
+    count = hot_plan.shape[0]
+    plans = list(itertools.combinations(range(n), count))
+    if len(plans) <= MAX_PLANS:
+        table = [0] * (1 << n)
+        for at, chosen in enumerate(plans):
+            table[sum(1 << e for e in chosen)] = at
+        which = jnp.asarray(table, jnp.int32)[jnp.sum(jnp.left_shift(1, hot_plan))]
+        branches = [
+            functools.partial(spread, n=n, sources=chosen, collective_id=1 + at)
+            for at, chosen in enumerate(plans)
+        ]
+        slots, scales = lax.switch(which, branches, quant_out, scale_out)
+        where = jnp.sum((hot_plan[None, :] < hot_plan[:, None]).astype(jnp.int32), axis=1)
+    else:
+        slots, scales = spread(quant_out, scale_out, n, tuple(range(n)), 1)
+        where = hot_plan
+    hot_values, replica_block_scales = place(where.astype(jnp.int32), hot_plan, slots, scales)
+    return quant_out, scale_out, hot_values, replica_block_scales
+
+
+def fits(n, reps, quant_in, scale_in, b_train, a_train):
+    slab = b_train[1] // reps
+    blocks = slab // BLOCK
+    wide = -(-blocks // n)
+    return (
+        quant_in[0] == n
+        and blocks * BLOCK == slab
+        and blocks % wide == 0
+        and (b_train[2] // reps) % 16 == 0
+        and a_train[2] % (n * BLOCK) == 0
+        and (slab // n) % 16 == 0
+    )
 
 
 def body(quant_in, scale_in, b_train, a_train, adapter_ranks, trainer_map, hot_plan):
@@ -74,6 +424,8 @@
 
 
 def solution(mesh):
+    n, reps = mesh.shape["ep"], mesh.shape["rep"]
+
     placed = (
         P("ep", "rep", None),
         P("ep", "rep", None),
@@ -83,15 +435,17 @@
         P(),
         P(),
     )
-    return jax.shard_map(
-        body,
-        mesh=mesh,
-        in_specs=placed,
-        out_specs=(
-            P("ep", "rep", None),
-            P("ep", "rep", None),
-            P(None, ("rep", "ep"), None),
-            P(None, "rep", None),
-        ),
-        check_vma=False,
-    )
+    outs = (
+        P("ep", "rep", None),
+        P("ep", "rep", None),
+        P(None, ("rep", "ep"), None),
+        P(None, "rep", None),
+    )
+
+    def run(quant_in, scale_in, b_train, a_train, adapter_ranks, trainer_map, hot_plan):
+        shapes = [v.shape for v in (quant_in, scale_in, b_train, a_train)]
+        local = functools.partial(kernel_body, n, reps) if fits(n, reps, *shapes) else body
+        step = jax.shard_map(local, mesh=mesh, in_specs=placed, out_specs=outs, check_vma=False)
+        return step(quant_in, scale_in, b_train, a_train, adapter_ranks, trainer_map, hot_plan)
+
+    return run

time: 532 us -> 215 us (0.40)
  the two profiles are of different devices: /device:TPU:0 before, /device:TPU:8 now
where the time goes in v1:
time: 215 us; the launch traced here: 213 us
  Pallas kernels  200 us (93%)
  local copies, waits for them, and re-layouts  11.9 us (6%)
    pallas_call x1, Pallas kernels, spread(): pl.pallas_call(functools.partial(hot_kernel, n, sources, piece), out_shap...  163 us
    pallas_call x1, Pallas kernels, exchange(): pl.pallas_call(functools.partial(exchange_kernel, n, reps, pieces, wide,...  25.5 us
    unnamed x17, local copies, waits for them, and re-layouts  10.7 us
    pallas_call x1, Pallas kernels, merge(): pl.pallas_call(merge_kernel, grid=(steps,), out_shape=(jax.ShapeDtypeStru...  8.39 us

profile of v1, /device:TPU:8, one launch (start us, length us, event | category | flops | bytes accessed | tf_op | source)
XLA Modules:
  0.0 212.9 jit_solution(8407276027711865815)
XLA Ops:
  0.6 1.2 dynamic_slice.3.rank
  1.9 0.8 select_reduce_fusion.inv
  2.6 0.7 copy.14.scale_in
  3.3 0.0 copy-start.2
  3.3 0.9 copy-done.2
  4.3 0.0 copy-start.4
  4.3 0.8 copy-done.4
  5.1 25.5 %exchange.1 = (bf16[4,16,1792]{2,1,0:T(8,128)(2,1)S(1)}, bf16[4,16,2048]{2,1,0:T(8,128)(2,1)S(1)}) custom-call(s32[8]{0:T(128)S(1)} %select_reduce_fusion.inv, bf16[1,16,7168]{2,1,0:T(8,128)(2,1)S(1)} %bitcast.4, bf16[1,16,2048]{2,1,0:T(8,128)(2,1)S(1)} %copy-done.4), custom_call_target="tpu_custom_call" | custom-call | tf_op jit(solution)/shard_map/exchange/pallas_call | solution.py:126
  30.6 0.0 copy-start
  30.6 3.1 %copy-done = bf16[1,1792,2048]{2,1,0:T(8,128)(2,1)S(1)} copy-done((bf16[1,1792,2048]{2,1,0:T(8,128)(2,1)S(1)}, bf16[1,1792,2048]{2,1,0:T(8,128)(2,1)}, u32[]{:S(2)}) %copy-start) | copy-done | bytes 7340056
  33.7 0.0 copy-start.6
  33.7 8.4 %merge.1 = (bf16[1,1792,2048]{2,1,0:T(8,128)(2,1)}, f32[1,14,16]{2,1,0:T(8,128)S(1)}) custom-call(s32[1]{0:T(128)} %dynamic_slice.3.rank, f32[1,14,16]{2,1,0:T(8,128)S(1)} %copy.14.scale_in, bf16[1,1792,2048]{2,1,0:T(8,128)(2,1)S(1)} %copy-done, bf16[64,1792]{1,0:T(8,128)(2,1)S(1)} %bitcast.5, bf16[64,2048]{1,0:T(8,128)(2,1)S(1)} %bitcast.3), custom_call_target="tpu_custom_call" | custom-call | tf_op jit(solution)/shard_map/merge/pallas_call | solution.py:187
  42.1 0.0 copy-start.5
  42.1 0.6 copy.15
  42.7 0.0 copy-done.5
  42.7 162.9 %spread.1 = (bf16[8,224,2048]{2,1,0:T(8,128)(2,1)}, f32[8,14,16]{2,1,0:T(8,128)}) custom-call(bf16[1,1792,2048]{2,1,0:T(8,128)(2,1)} %get-tuple-element.24.quant, f32[1,14,16]{2,1,0:T(8,128)} %copy-done.5), custom_call_target="tpu_custom_call" | custom-call | tf_op jit(solution)/shard_map/spread/pallas_call | solution.py:263
  205.6 0.0 copy-done.6
  205.6 0.0 copy-start.1
  205.6 3.1 %copy-done.1 = bf16[8,224,2048]{2,1,0:T(8,128)(2,1)S(1)} copy-done((bf16[8,224,2048]{2,1,0:T(8,128)(2,1)S(1)}, bf16[8,224,2048]{2,1,0:T(8,128)(2,1)}, u32[]{:S(2)}) %copy-start.1) | copy-done | bytes 7340056
  208.7 0.0 copy-start.3
  208.7 0.8 copy-done.3
  209.5 2.8 %place.1 = (bf16[4,224,2048]{2,1,0:T(8,128)(2,1)}, f32[4,14,16]{2,1,0:T(8,128)S(1)}) custom-call(s32[4]{0:T(128)S(1)} %copy-done.6, s32[4]{0:T(128)S(1)} %copy-done.6, bf16[8,224,2048]{2,1,0:T(8,128)(2,1)S(1)} %copy-done.1, f32[8,14,16]{2,1,0:T(8,128)S(1)} %copy-done.3), custom_call_target="tpu_custom_call" | custom-call | tf_op jit(solution)/shard_map/place/pallas_call | solution.py:295
  212.3 0.6 copy.16
Async XLA Ops:
  3.3 0.9 copy-start.2
  4.3 0.8 copy-start.4
  30.6 3.1 %copy-start = (bf16[1,1792,2048]{2,1,0:T(8,128)(2,1)S(1)}, bf16[1,1792,2048]{2,1,0:T(8,128)(2,1)}, u32[]{:S(2)}) copy-start(bf16[1,1792,2048]{2,1,0:T(8,128)(2,1)} %quant_in.1) | copy-start | bytes 22020100
  33.7 171.9 %copy-start.6 = (s32[4]{0:T(128)S(1)}, s32[4]{0:T(128)}, u32[]{:S(2)}) copy-start(s32[4]{0:T(128)} %plan.1) | copy-start | bytes 52
  42.1 0.6 copy-start.5
  205.6 3.1 %copy-start.1 = (bf16[8,224,2048]{2,1,0:T(8,128)(2,1)S(1)}, bf16[8,224,2048]{2,1,0:T(8,128)(2,1)}, u32[]{:S(2)}) copy-start(bf16[8,224,2048]{2,1,0:T(8,128)(2,1)} %get-tuple-element.16.held) | copy-start | bytes 22020100
  208.7 0.8 copy-start.3

commit v2 on v1

--- a/solution.py
+++ b/solution.py
@@ -14,7 +14,7 @@
 
 
 EPS = 1e-06
-MAX_PLANS = 0
+MAX_PLANS = 128
 MESH = pl.DeviceIdType.MESH
 
 

time: 215 us -> 216 us (level)
  local copies, waits for them, and re-layouts: 11.9 us -> 8.61 us
  between operations: 0.68 us -> 3.27 us
    unnamed x17 -> x13, local copies, waits for them, and re-layouts: 10.7 us -> 6.79 us
where the time goes in v2:
time: 216 us; the launch traced here: 214 us
  Pallas kernels  200 us (93%)
  local copies, waits for them, and re-layouts  8.61 us (4%)
  between operations  3.27 us (2%)
    pallas_call x1, Pallas kernels, spread(): pl.pallas_call(functools.partial(hot_kernel, n, sources, piece), out_shap...  162 us
    pallas_call x1, Pallas kernels, exchange(): pl.pallas_call(functools.partial(exchange_kernel, n, reps, pieces, wide,...  25.5 us
    pallas_call x1, Pallas kernels, merge(): pl.pallas_call(merge_kernel, grid=(steps,), out_shape=(jax.ShapeDtypeStru...  8.39 us
    unnamed x13, local copies, waits for them, and re-layouts  6.79 us
    pallas_call x1, Pallas kernels, place(): pl.pallas_call(place_kernel, grid_spec=pltpu.PrefetchScalarGridSpec(num_s...  5 us

profile of v2, /device:TPU:8, one launch (start us, length us, event | category | flops | bytes accessed | tf_op | source)
XLA Modules:
  0.0 214.5 jit_solution(328600003519994689)
XLA Ops:
  0.6 1.2 dynamic_slice.6.rank
  1.9 0.8 select_reduce_fusion.inv
  2.6 0.0 copy-start.1
  2.7 0.9 copy-done.1
  3.6 0.0 copy-start.2
  3.6 0.8 copy-done.2
  4.4 25.5 %exchange.1 = (bf16[4,16,1792]{2,1,0:T(8,128)(2,1)S(1)}, bf16[4,16,2048]{2,1,0:T(8,128)(2,1)S(1)}) custom-call(s32[8]{0:T(128)S(1)} %select_reduce_fusion.inv, bf16[1,16,7168]{2,1,0:T(8,128)(2,1)S(1)} %bitcast.5, bf16[1,16,2048]{2,1,0:T(8,128)(2,1)S(1)} %copy-done.2), custom_call_target="tpu_custom_call" | custom-call | tf_op jit(solution)/shard_map/exchange/pallas_call | solution.py:126
  29.9 0.7 copy.15.scale_in
  30.6 0.0 copy-start
  30.6 3.1 %copy-done = bf16[1,1792,2048]{2,1,0:T(8,128)(2,1)S(1)} copy-done((bf16[1,1792,2048]{2,1,0:T(8,128)(2,1)S(1)}, bf16[1,1792,2048]{2,1,0:T(8,128)(2,1)}, u32[]{:S(2)}) %copy-start) | copy-done | bytes 7340056
  33.7 0.0 copy-start.3
  33.7 0.0 copy-start.4
  33.7 8.4 %merge.1 = (bf16[1,1792,2048]{2,1,0:T(8,128)(2,1)}, f32[1,14,16]{2,1,0:T(8,128)S(1)}) custom-call(s32[1]{0:T(128)} %dynamic_slice.6.rank, f32[1,14,16]{2,1,0:T(8,128)S(1)} %copy.15.scale_in, bf16[1,1792,2048]{2,1,0:T(8,128)(2,1)S(1)} %copy-done, bf16[64,1792]{1,0:T(8,128)(2,1)S(1)} %bitcast.6, bf16[64,2048]{1,0:T(8,128)(2,1)S(1)} %bitcast.4), custom_call_target="tpu_custom_call" | custom-call | tf_op jit(solution)/shard_map/merge/pallas_call | solution.py:187
  42.1 0.0 copy-done.3
  42.1 0.6 shift-left_reduce_fusion
  44.7 0.0 copy-done.4
  44.7 0.6 dynamic_slice.7
  45.9 162.2 %conditional.1 = ((bf16[4,224,2048]{2,1,0:T(8,128)(2,1)}, f32[8,14,16]{2,1,0:T(8,128)S(1)})) conditional(s32[]{:T(128)} %bitcast.3, (bf16[1,1792,2048]{2,1,0:T(8,128)(2,1)}, f32[1,14,16]{2,1,0:T(8,128)S(1)}) %merge.1, (bf16[1,1792,2048]{2,1,0:T(8,128)(2,1)}, f32[1,14,16]{2,1,0:T(8,128)S(1)}) %merge.1, ...), branch_computations={%region_3.4_spmd, %region_4.5_spmd, %region_5.6_spmd, %region_6.7_... | conditional | bytes 8 | solution.py:340
  46.0 161.6 %spread.74 = (bf16[4,224,2048]{2,1,0:T(8,128)(2,1)}, f32[8,14,16]{2,1,0:T(8,128)S(1)}) custom-call(bf16[1,1792,2048]{2,1,0:T(8,128)(2,1)} %get-tuple-element.288.quant, f32[1,14,16]{2,1,0:T(8,128)S(1)} %get-tuple-element.289.scale), custom_call_target="tpu_custom_call" | custom-call | tf_op jit(solution)/shard_map/cond/branch_4_fun/spread/pallas_call | solution.py:263
  208.1 0.2 convert_reduce_fusion.where
  208.3 5.0 %place.1 = (bf16[4,224,2048]{2,1,0:T(8,128)(2,1)}, f32[4,14,16]{2,1,0:T(8,128)S(1)}) custom-call(s32[4]{0:T(128)S(1)} %convert_reduce_fusion.where, s32[4]{0:T(128)S(1)} %copy-done.3, bf16[4,224,2048]{2,1,0:T(8,128)(2,1)} %get-tuple-element.436.held, f32[8,14,16]{2,1,0:T(8,128)S(1)} %get-tuple-element.437.scales), custom_call_target="tpu_custom_call" | custom-call | tf_op jit(solution)/shard_map/place/pallas_call | solution.py:295
  213.3 0.6 copy.17
  213.9 0.6 copy.16
Async XLA Ops:
  2.6 0.9 copy-start.1
  3.6 0.8 copy-start.2
  30.6 3.1 %copy-start = (bf16[1,1792,2048]{2,1,0:T(8,128)(2,1)S(1)}, bf16[1,1792,2048]{2,1,0:T(8,128)(2,1)}, u32[]{:S(2)}) copy-start(bf16[1,1792,2048]{2,1,0:T(8,128)(2,1)} %quant_in.1) | copy-start | bytes 22020100
  33.7 8.4 %copy-start.3 = (s32[4]{0:T(128)S(1)}, s32[4]{0:T(128)}, u32[]{:S(2)}) copy-start(s32[4]{0:T(128)} %plan.1) | copy-start | bytes 52
  33.7 11.0 %copy-start.4 = (s32[256]{0:T(256)S(1)}, s32[256]{0:T(256)}, u32[]{:S(2)}) copy-start(s32[256]{0:T(256)} %constant.21.clone) | copy-start | bytes 3076

commit v3 on v2

--- a/solution.py
+++ b/solution.py
@@ -208,63 +208,141 @@
     )(rank, scale_in, quant_in, bt, a)
 
 
-def hot_kernel(n, sources, piece, quant, scale, slots, scales, send, recv, ssend, srecv):
+def hot_kernel(n, sources, piece, chunks, quant, scale, slots, scales, hold,
+               send, recv, forward_send, hold_recv, scale_send, scale_recv):
     ep = lax.axis_index("ep")
+    line = lax.rem(ep, 2)
+    spot = lax.div(ep, 2)
+    half = n // 2
+    partner = ep + 1 - 2 * line
+    size = piece // chunks
+
+    def source(e):
+        hit = functools.reduce(jnp.logical_or, [e == s for s in sources])
+        slot = sum((e > s).astype(jnp.int32) for s in sources)
+        return hit, jnp.minimum(slot, len(sources) - 1)
+
+    mine, slot = source(ep)
+    theirs, partner_slot = source(partner)
+
+    def at(de):
+        return {"ep": lax.rem(ep + de, n)}
+
     barrier = pltpu.get_barrier_semaphore()
-    for de in range(1, n):
-        pl.semaphore_signal(
-            barrier, inc=1, device_id={"ep": lax.rem(ep + de, n)}, device_id_type=MESH
+
+    @pl.loop(1, n)
+    def _(de):
+        pl.semaphore_signal(barrier, inc=1, device_id=at(de), device_id_type=MESH)
+
+    pl.semaphore_wait(barrier, n - 1)
+
+    def remote(src, dst, send_sem, recv_sem, p):
+        return pltpu.make_async_remote_copy(
+            src_ref=src, dst_ref=dst, send_sem=send_sem, recv_sem=recv_sem,
+            device_id={"ep": p}, device_id_type=MESH,
         )
-    pl.semaphore_wait(barrier, n - 1)
+
+    def far(i):
+        if half == 4:
+            step = 2 if i == 0 else (3 - 2 * lax.rem(spot, 2) if i == 1 else 1 + 2 * lax.rem(spot, 2))
+        else:
+            step = i + 1
+        return lax.rem(spot + step, half)
+
+    def piece_rows(p):
+        return quant.at[0, pl.ds(pl.multiple_of(p * piece, 16), piece)]
+
+    def chunk(c):
+        return pl.ds(pl.multiple_of(c * size, 16), size)
+
+    def direct(p, sem):
+        return remote(piece_rows(p), slots.at[slot], send.at[sem], recv.at[slot], p)
+
+    def along(i):
+        return direct(far(i) * 2 + line, i)
+
+    def lend(i, c):
+        p = far(i) * 2 + 1 - line
+        rows = pl.ds(pl.multiple_of(p * piece + c * size, 16), size)
+        return remote(
+            quant.at[0, rows], hold.at[i, chunk(c)], send.at[half + i], hold_recv.at[i, c], partner
+        )
+
+    def forward(i, c):
+        return remote(
+            hold.at[i, chunk(c)], slots.at[partner_slot, chunk(c)], forward_send.at[i],
+            recv.at[partner_slot], far(i) * 2 + line,
+        )
 
     def scale_copy(de):
         return pltpu.make_async_remote_copy(
-            src_ref=scale, dst_ref=scales.at[pl.ds(ep, 1)], send_sem=ssend.at[de],
-            recv_sem=srecv.at[ep], device_id={"ep": lax.rem(ep + de, n)}, device_id_type=MESH,
+            src_ref=scale, dst_ref=scales.at[pl.ds(ep, 1)], send_sem=scale_send.at[de],
+            recv_sem=scale_recv.at[ep], device_id=at(de), device_id_type=MESH,
         )
 
-    def piece_copy(k, p):
-        return pltpu.make_async_remote_copy(
-            src_ref=quant.at[0, pl.ds(p * piece, piece)], dst_ref=slots.at[k],
-            send_sem=send.at[p], recv_sem=recv.at[k], device_id={"ep": p}, device_id_type=MESH,
-        )
-
-    def own_copy(k, p):
-        return pltpu.make_async_copy(quant.at[0, pl.ds(p * piece, piece)], slots.at[k], recv.at[k])
-
-    own_scale = pltpu.make_async_copy(scale, scales.at[pl.ds(ep, 1)], srecv.at[ep])
-    own_scale.start()
-    for de in range(1, n):
+    own = pltpu.make_async_copy(piece_rows(ep), slots.at[slot], recv.at[slot])
+
+    @pl.when(mine)
+    def _():
+        for i in range(half - 1):
+            @pl.loop(0, chunks)
+            def _(c):
+                lend(i, c).start()
+
+            along(i).start()
+        direct(partner, half - 1).start()
+        own.start()
+
+    pltpu.make_async_copy(scale, scales.at[pl.ds(ep, 1)], scale_recv.at[ep]).start()
+
+    @pl.loop(1, n)
+    def _(de):
         scale_copy(de).start()
-    for k, e in enumerate(sources):
-        @pl.when(ep == e)
-        def _():
-            for p in range(n):
-                if p != e:
-                    piece_copy(k, p).start()
-            own_copy(k, e).start()
-    for k in range(len(sources)):
+
+    @pl.when(theirs)
+    def _():
+        for i in range(half - 1):
+            @pl.loop(0, chunks)
+            def _(c):
+                pltpu.make_async_copy(
+                    hold.at[i, chunk(c)], hold.at[i, chunk(c)], hold_recv.at[i, c]
+                ).wait()
+                forward(i, c).start()
+
+    @pl.loop(0, n)
+    def _(s):
+        pltpu.make_async_copy(scales.at[pl.ds(s, 1)], scales.at[pl.ds(s, 1)], scale_recv.at[s]).wait()
+
+    @pl.loop(1, n)
+    def _(de):
+        scale_copy(de).wait_send()
+
+    @pl.loop(0, len(sources))
+    def _(k):
         pltpu.make_async_copy(slots.at[k], slots.at[k], recv.at[k]).wait()
-    for k, e in enumerate(sources):
-        @pl.when(ep == e)
-        def _():
-            for p in range(n):
-                if p != e:
-                    piece_copy(k, p).wait_send()
-    for s in range(n):
-        pltpu.make_async_copy(scales.at[pl.ds(s, 1)], scales.at[pl.ds(s, 1)], srecv.at[s]).wait()
-    for de in range(1, n):
-        scale_copy(de).wait_send()
+
+    @pl.when(theirs)
+    def _():
+        for i in range(half - 1):
+            pltpu.make_async_copy(hold.at[i], hold.at[i], forward_send.at[i]).wait()
+
+    @pl.when(mine)
+    def _():
+        for i in range(2 * half - 1):
+            pltpu.make_async_copy(slots.at[slot], slots.at[slot], send.at[i]).wait()
 
 
 def spread(quant, scale, n, sources, collective_id):
     piece = quant.shape[1] // n
+    chunks = next(c for c in (7, 5, 4, 3, 2, 1) if piece % (16 * c) == 0)
+    half = n // 2
     dma = pltpu.SemaphoreType.DMA
     return pl.pallas_call(
-        functools.partial(hot_kernel, n, sources, piece),
+        functools.partial(hot_kernel, n, sources, piece, chunks),
         out_shape=(
             jax.ShapeDtypeStruct((len(sources), piece, quant.shape[2]), quant.dtype),
             jax.ShapeDtypeStruct((n,) + scale.shape[1:], scale.dtype),
+            jax.ShapeDtypeStruct((half - 1, piece, quant.shape[2]), quant.dtype),
         ),
         in_specs=[
             pl.BlockSpec(memory_space=pl.ANY),
@@ -273,11 +351,15 @@
         out_specs=(
             pl.BlockSpec(memory_space=pl.ANY),
             pl.BlockSpec(memory_space=pltpu.VMEM),
-        ),
-        scratch_shapes=[dma((n,)), dma((len(sources),)), dma((n,)), dma((n,))],
+            pl.BlockSpec(memory_space=pl.ANY),
+        ),
+        scratch_shapes=[
+            dma((2 * half,)), dma((len(sources),)), dma((half,)), dma((half, chunks)),
+            dma((n,)), dma((n,)),
+        ],
         compiler_params=pltpu.CompilerParams(collective_id=collective_id, has_side_effects=True),
         name="spread",
-    )(quant, scale)
+    )(quant, scale)[:2]
 
 
 def place_kernel(where, plan, held, scales, values, picked):
@@ -352,6 +434,8 @@
     wide = -(-blocks // n)
     return (
         quant_in[0] == n
+        and n % 2 == 0
+        and n > 2
         and blocks * BLOCK == slab
         and blocks % wide == 0
         and (b_train[2] // reps) % 16 == 0

time: 216 us -> 178 us (0.82)
  Pallas kernels: 200 us -> 164 us
    pallas_call x1, Pallas kernels: 162 us -> 125 us  [spread(): pl.pallas_call(functools.partial(hot_kernel, n, sources, piece, chunks),...]
where the time goes in v3:
time: 178 us; the launch traced here: 177 us
  Pallas kernels  164 us (92%)
  local copies, waits for them, and re-layouts  8.61 us (5%)
  between operations  3.27 us (2%)
    pallas_call x1, Pallas kernels, spread(): pl.pallas_call(functools.partial(hot_kernel, n, sources, piece, chunks),...  125 us
    pallas_call x1, Pallas kernels, exchange(): pl.pallas_call(functools.partial(exchange_kernel, n, reps, pieces, wide,...  25.5 us
    pallas_call x1, Pallas kernels, merge(): pl.pallas_call(merge_kernel, grid=(steps,), out_shape=(jax.ShapeDtypeStru...  8.39 us
    unnamed x13, local copies, waits for them, and re-layouts  6.79 us
    pallas_call x1, Pallas kernels, place(): pl.pallas_call(place_kernel, grid_spec=pltpu.PrefetchScalarGridSpec(num_s...  5 us

profile of v3, /device:TPU:8, one launch (start us, length us, event | category | flops | bytes accessed | tf_op | source)
XLA Modules:
  0.0 177.5 jit_solution(15537136740805305990)
XLA Ops:
  0.6 1.2 dynamic_slice.6.rank
  1.9 0.8 select_reduce_fusion.inv
  2.6 0.0 copy-start.1
  2.7 0.9 copy-done.1
  3.6 0.0 copy-start.2
  3.6 0.8 copy-done.2
  4.4 25.5 %exchange.1 = (bf16[4,16,1792]{2,1,0:T(8,128)(2,1)S(1)}, bf16[4,16,2048]{2,1,0:T(8,128)(2,1)S(1)}) custom-call(s32[8]{0:T(128)S(1)} %select_reduce_fusion.inv, bf16[1,16,7168]{2,1,0:T(8,128)(2,1)S(1)} %bitcast.5, bf16[1,16,2048]{2,1,0:T(8,128)(2,1)S(1)} %copy-done.2), custom_call_target="tpu_custom_call" | custom-call | tf_op jit(solution)/shard_map/exchange/pallas_call | solution.py:126
  29.9 0.7 copy.15.scale_in
  30.6 0.0 copy-start
  30.6 3.1 %copy-done = bf16[1,1792,2048]{2,1,0:T(8,128)(2,1)S(1)} copy-done((bf16[1,1792,2048]{2,1,0:T(8,128)(2,1)S(1)}, bf16[1,1792,2048]{2,1,0:T(8,128)(2,1)}, u32[]{:S(2)}) %copy-start) | copy-done | bytes 7340056
  33.7 0.0 copy-start.3
  33.7 0.0 copy-start.4
  33.7 8.4 %merge.1 = (bf16[1,1792,2048]{2,1,0:T(8,128)(2,1)}, f32[1,14,16]{2,1,0:T(8,128)S(1)}) custom-call(s32[1]{0:T(128)} %dynamic_slice.6.rank, f32[1,14,16]{2,1,0:T(8,128)S(1)} %copy.15.scale_in, bf16[1,1792,2048]{2,1,0:T(8,128)(2,1)S(1)} %copy-done, bf16[64,1792]{1,0:T(8,128)(2,1)S(1)} %bitcast.6, bf16[64,2048]{1,0:T(8,128)(2,1)S(1)} %bitcast.4), custom_call_target="tpu_custom_call" | custom-call | tf_op jit(solution)/shard_map/merge/pallas_call | solution.py:187
  42.1 0.0 copy-done.3
  42.1 0.6 shift-left_reduce_fusion
  44.7 0.0 copy-done.4
  44.7 0.6 dynamic_slice.7
  45.9 125.2 %conditional.1 = (bf16[4,224,2048]{2,1,0:T(8,128)(2,1)}, f32[8,14,16]{2,1,0:T(8,128)S(1)}) conditional(s32[]{:T(128)} %bitcast.3, (bf16[1,1792,2048]{2,1,0:T(8,128)(2,1)}, f32[1,14,16]{2,1,0:T(8,128)S(1)}) %merge.1, (bf16[1,1792,2048]{2,1,0:T(8,128)(2,1)}, f32[1,14,16]{2,1,0:T(8,128)S(1)}) %merge.1, ...), branch_computations={%region_3.4_spmd, %region_4.5_spmd, %region_5.6_spmd, %region_6.7_... | conditional | bytes 16 | solution.py:422
  46.2 124.7 %spread.102 = (bf16[4,224,2048]{2,1,0:T(8,128)(2,1)}, f32[8,14,16]{2,1,0:T(8,128)S(1)}, bf16[3,224,2048]{2,1,0:T(8,128)(2,1)}) custom-call(bf16[1,1792,2048]{2,1,0:T(8,128)(2,1)} %get-tuple-element.408.quant, f32[1,14,16]{2,1,0:T(8,128)S(1)} %get-tuple-element.409.scale), custom_call_target="tpu_custom_call" | custom-call | tf_op jit(solution)/shard_map/cond/branch_32_fun/spread/pallas_call | solution.py:340
  171.1 0.2 convert_reduce_fusion.where
  171.3 5.0 %place.1 = (bf16[4,224,2048]{2,1,0:T(8,128)(2,1)}, f32[4,14,16]{2,1,0:T(8,128)S(1)}) custom-call(s32[4]{0:T(128)S(1)} %convert_reduce_fusion.where, s32[4]{0:T(128)S(1)} %copy-done.3, bf16[4,224,2048]{2,1,0:T(8,128)(2,1)} %get-tuple-element.576.held, f32[8,14,16]{2,1,0:T(8,128)S(1)} %get-tuple-element.577.scales), custom_call_target="tpu_custom_call" | custom-call | tf_op jit(solution)/shard_map/place/pallas_call | solution.py:377
  176.3 0.6 copy.17
  176.9 0.6 copy.16
Async XLA Ops:
  2.6 0.9 copy-start.1
  3.6 0.8 copy-start.2
  30.6 3.1 %copy-start = (bf16[1,1792,2048]{2,1,0:T(8,128)(2,1)S(1)}, bf16[1,1792,2048]{2,1,0:T(8,128)(2,1)}, u32[]{:S(2)}) copy-start(bf16[1,1792,2048]{2,1,0:T(8,128)(2,1)} %quant_in.1) | copy-start | bytes 22020100
  33.7 8.4 %copy-start.3 = (s32[4]{0:T(128)S(1)}, s32[4]{0:T(128)}, u32[]{:S(2)}) copy-start(s32[4]{0:T(128)} %plan.1) | copy-start | bytes 52
  33.7 11.0 %copy-start.4 = (s32[256]{0:T(256)S(1)}, s32[256]{0:T(256)}, u32[]{:S(2)}) copy-start(s32[256]{0:T(256)} %constant.21.clone) | copy-start | bytes 3076

commit v4 on v3

--- a/solution.py
+++ b/solution.py
@@ -20,7 +20,7 @@
 
 def exchange_kernel(n, reps, pieces, wide, cols, inv, b_ref, a_ref, bt_out, a_out,
                     b_mid, a_mid, b_stage, a_stage,
-                    sb1, rb1, sa1, ra1, sb2, rb2, sa2, ra2):
+                    sb1, rb1, sa1, ra1, sb2, rb2, sa2, ra2, sa3, ra3):
     ep = lax.axis_index("ep")
     rep = lax.axis_index("rep")
     slab = pieces * wide
@@ -71,10 +71,13 @@
     for d in range(n):
         a_stage[d] = a_mid[inv[d]]
 
-    def a_second(de, dr):
+    def a_second(de):
         d = lax.rem(ep + de, n)
         dst = a_out.at[rep, :, pl.ds(pl.multiple_of(ep * cols, cols), cols)]
-        return move(not (de or dr), a_stage.at[d], dst, sa2.at[de, dr], ra2.at[ep, rep], de, dr)
+        return move(de == 0, a_stage.at[d], dst, sa2.at[de], ra2.at[ep], de, 0)
+
+    def a_third(dr):
+        return move(False, a_out.at[rep], a_out.at[rep], sa3.at[dr], ra3.at[rep], 0, dr)
 
     def b_second(de):
         d = lax.rem(ep + de, n)
@@ -82,8 +85,8 @@
         dst = bt_out.at[:, :, pl.ds(pl.multiple_of(here * wide, wide), wide)]
         return move(de == 0, b_stage.at[d], dst, sb2.at[de], rb2.at[ep], de, 0)
 
-    for de, dr in order:
-        a_second(de, dr).start()
+    for de in reversed(range(n)):
+        a_second(de).start()
 
     @pl.when(ep < pieces)
     def _():
@@ -96,9 +99,13 @@
             b_second(de).start()
 
     for j in range(n):
-        for q in range(reps):
-            dst = a_out.at[q, :, pl.ds(j * cols, cols)]
-            pltpu.make_async_copy(dst, dst, ra2.at[j, q]).wait()
+        dst = a_out.at[rep, :, pl.ds(j * cols, cols)]
+        pltpu.make_async_copy(dst, dst, ra2.at[j]).wait()
+    for dr in range(1, reps):
+        a_third(dr).start()
+    for dr in range(1, reps):
+        q = lax.rem(rep + dr, reps)
+        pltpu.make_async_copy(a_out.at[q], a_out.at[q], ra3.at[q]).wait()
     for j in range(pieces):
         dst = bt_out.at[:, :, pl.ds(j * wide, wide)]
         pltpu.make_async_copy(dst, dst, rb2.at[j]).wait()
@@ -106,9 +113,11 @@
         if de or dr:
             j, copy = b_first(de, dr)
             pl.when(j < pieces)(copy.wait_send)
-            a_second(de, dr).wait_send()
+    for dr in range(1, reps):
+        a_third(dr).wait_send()
     for de in range(1, n):
         a_first(de).wait_send()
+        a_second(de).wait_send()
         copy = b_second(de)
         pl.when(ep < pieces)(copy.wait_send)
 
@@ -131,8 +140,8 @@
         ),
         in_specs=[
             pl.BlockSpec(memory_space=pltpu.SMEM),
-            pl.BlockSpec(memory_space=pltpu.VMEM),
-            pl.BlockSpec(memory_space=pltpu.VMEM),
+            pl.BlockSpec(memory_space=pl.ANY),
+            pl.BlockSpec(memory_space=pl.ANY),
         ],
         out_specs=(pl.BlockSpec(memory_space=pltpu.VMEM),) * 2,
         scratch_shapes=[
@@ -141,23 +150,23 @@
             pltpu.VMEM((n, reps, ranks, wide), bf16),
             pltpu.VMEM((n, ranks, cols), bf16),
             dma((n, reps)), dma((n, reps)), dma((n,)), dma((n,)),
-            dma((n,)), dma((n,)), dma((n, reps)), dma((n, reps)),
+            dma((n,)), dma((n,)), dma((n,)), dma((n,)), dma((reps,)), dma((reps,)),
         ],
         compiler_params=pltpu.CompilerParams(
-            collective_id=0, has_side_effects=True, vmem_limit_bytes=32 << 20
+            collective_id=0, has_side_effects=True
         ),
         name="exchange",
     )(inv, jnp.swapaxes(b_train, 1, 2), a_train)
 
 
-def merge_kernel(rank, scale_in, quant_in, bt, a, quant_out, scale_out, live):
+def merge_kernel(ranks, scale_in, quant_in, bt, a, quant_out, scale_out, live):
     step = pl.program_id(0)
     blocks = quant_in.shape[1] // BLOCK
     col_blocks = quant_in.shape[2] // BLOCK
 
     @pl.when(step == 0)
     def _():
-        keep = lax.broadcasted_iota(jnp.int32, live.shape, 0) < rank[0]
+        keep = lax.broadcasted_iota(jnp.int32, live.shape, 0) < ranks[lax.axis_index("ep")]
         live[...] = jnp.where(keep, a[...].astype(jnp.float32), 0.0).astype(jnp.bfloat16)
 
     lane = lax.broadcasted_iota(jnp.int32, (1, col_blocks), 1)
@@ -178,7 +187,7 @@
         scale_out[0, pl.ds(step * blocks + i, 1), :] = found
 
 
-def merge(rank, scale_in, quant_in, bt, a):
+def merge(ranks, scale_in, quant_in, bt, a):
     _, rows, features = quant_in.shape
     total = rows // BLOCK
     blocks = 2 if total % 2 == 0 else 1
@@ -203,9 +212,8 @@
             pl.BlockSpec(scale_in.shape, lambda i: (0, 0, 0)),
         ),
         scratch_shapes=[pltpu.VMEM(a.shape, jnp.bfloat16)],
-        compiler_params=pltpu.CompilerParams(vmem_limit_bytes=32 << 20),
         name="merge",
-    )(rank, scale_in, quant_in, bt, a)
+    )(ranks, scale_in, quant_in, bt, a)
 
 
 def hot_kernel(n, sources, piece, chunks, quant, scale, slots, scales, hold,
@@ -365,7 +373,7 @@
 def place_kernel(where, plan, held, scales, values, picked):
     values[...] = held[...]
 
-    @pl.when(pl.program_id(0) == 0)
+    @pl.when((pl.program_id(0) == 0) & (pl.program_id(1) == 0))
     def _():
         for k in range(picked.shape[0]):
             picked[k] = scales[plan[k]]
@@ -373,32 +381,31 @@
 
 def place(where, plan, slots, scales):
     count = plan.shape[0]
-    block = (1,) + slots.shape[1:]
+    parts = 2
+    block = (1, slots.shape[1] // parts, slots.shape[2])
     return pl.pallas_call(
         place_kernel,
         grid_spec=pltpu.PrefetchScalarGridSpec(
             num_scalar_prefetch=2,
-            grid=(count,),
+            grid=(count, parts),
             in_specs=[
-                pl.BlockSpec(block, lambda k, where, plan: (where[k], 0, 0)),
-                pl.BlockSpec(scales.shape, lambda k, where, plan: (0, 0, 0)),
+                pl.BlockSpec(block, lambda k, h, where, plan: (where[k], h, 0)),
+                pl.BlockSpec(scales.shape, lambda k, h, where, plan: (0, 0, 0)),
             ],
             out_specs=[
-                pl.BlockSpec(block, lambda k, where, plan: (k, 0, 0)),
-                pl.BlockSpec((count,) + scales.shape[1:], lambda k, where, plan: (0, 0, 0)),
+                pl.BlockSpec(block, lambda k, h, where, plan: (k, h, 0)),
+                pl.BlockSpec((count,) + scales.shape[1:], lambda k, h, where, plan: (0, 0, 0)),
             ],
         ),
         out_shape=(
             jax.ShapeDtypeStruct((count,) + slots.shape[1:], slots.dtype),
             jax.ShapeDtypeStruct((count,) + scales.shape[1:], scales.dtype),
         ),
-        compiler_params=pltpu.CompilerParams(vmem_limit_bytes=32 << 20),
         name="place",
     )(where, plan, slots, scales)
 
 
 def kernel_body(n, reps, quant_in, scale_in, b_train, a_train, adapter_ranks, trainer_map, hot_plan):
-    owner = lax.axis_index("ep")
     serving = jnp.arange(n, dtype=jnp.int32)
     inv = jnp.sum(
         jnp.where(trainer_map[None, :] == serving[:, None], serving[None, :], 0), axis=1
@@ -406,8 +413,7 @@
     bt, a = exchange(inv, b_train, a_train, n, reps)
     bt = bt.reshape(-1, bt.shape[2])
     a = a.reshape(-1, a.shape[2])
-    rank = lax.dynamic_slice_in_dim(adapter_ranks, owner, 1, 0)
-    quant_out, scale_out = merge(rank, scale_in, quant_in, bt, a)
+    quant_out, scale_out = merge(adapter_ranks, scale_in, quant_in, bt, a)
     count = hot_plan.shape[0]
     plans = list(itertools.combinations(range(n), count))
     if len(plans) <= MAX_PLANS:
@@ -440,7 +446,7 @@
         and blocks % wide == 0
         and (b_train[2] // reps) % 16 == 0
         and a_train[2] % (n * BLOCK) == 0
-        and (slab // n) % 16 == 0
+        and (slab // n) % 32 == 0
     )
 
 

time: 178 us -> 178 us (level)
  local copies, waits for them, and re-layouts: 8.61 us -> 4.55 us
    unnamed x13 -> x5, local copies, waits for them, and re-layouts: 6.79 us -> 3.28 us
    pallas_call x1, Pallas kernels: 8.39 us -> 10.6 us  [merge(): pl.pallas_call(merge_kernel, grid=(steps,), out_shape=(jax.ShapeDtypeStru...]
    pallas_call x1, Pallas kernels: 5 us -> 7.05 us  [place(): pl.pallas_call(place_kernel, grid_spec=pltpu.PrefetchScalarGridSpec(num_s...]
where the time goes in v4:
time: 178 us; the launch traced here: 176 us
  Pallas kernels  165 us (93%)
  local copies, waits for them, and re-layouts  4.55 us (3%)
  other arithmetic  3.27 us (2%)
  between operations  3.26 us (2%)
    pallas_call x1, Pallas kernels, spread(): pl.pallas_call(functools.partial(hot_kernel, n, sources, piece, chunks),...  123 us
    pallas_call x1, Pallas kernels, exchange(): pl.pallas_call(functools.partial(exchange_kernel, n, reps, pieces, wide,...  23.8 us
    pallas_call x1, Pallas kernels, merge(): pl.pallas_call(merge_kernel, grid=(steps,), out_shape=(jax.ShapeDtypeStru...  10.6 us
    pallas_call x1, Pallas kernels, place(): pl.pallas_call(place_kernel, grid_spec=pltpu.PrefetchScalarGridSpec(num_s...  7.05 us

profile of v4, /device:TPU:8, one launch (start us, length us, event | category | flops | bytes accessed | tf_op | source)
XLA Modules:
  0.0 175.9 jit_solution(17040210468770095136)
XLA Ops:
  0.6 1.3 shift-left_reduce_fusion
  3.9 1.3 dynamic_slice.3
  5.8 1.3 select_reduce_fusion.inv
  7.1 23.8 %exchange.1 = (bf16[4,16,1792]{2,1,0:T(8,128)(2,1)}, bf16[4,16,2048]{2,1,0:T(8,128)(2,1)}) custom-call(s32[8]{0:T(128)} %select_reduce_fusion.inv, bf16[1,16,7168]{2,1,0:T(8,128)(2,1)} %bitcast.5, bf16[1,16,2048]{2,1,0:T(8,128)(2,1)} %a_ref.1), custom_call_target="tpu_custom_call" | custom-call | tf_op jit(solution)/shard_map/exchange/pallas_call | solution.py:135
  30.9 1.3 copy.15.scale_in
  32.2 10.6 %merge.1 = (bf16[1,1792,2048]{2,1,0:T(8,128)(2,1)}, f32[1,14,16]{2,1,0:T(8,128)S(1)}) custom-call(s32[8]{0:T(128)} %ranks.1, f32[1,14,16]{2,1,0:T(8,128)} %copy.15.scale_in, bf16[1,1792,2048]{2,1,0:T(8,128)(2,1)} %quant_in.1, bf16[64,1792]{1,0:T(8,128)(2,1)} %bitcast.6, bf16[64,2048]{1,0:T(8,128)(2,1)} %bitcast.4), custom_call_target="tpu_custom_call" | custom-call | tf_op jit(solution)/shard_map/merge/pallas_call | solution.py:196
  42.7 0.0 copy-start
  42.7 123.4 %conditional.1 = (bf16[4,224,2048]{2,1,0:T(8,128)(2,1)}, f32[8,14,16]{2,1,0:T(8,128)S(1)}) conditional(s32[]{:T(128)} %bitcast.3, (bf16[1,1792,2048]{2,1,0:T(8,128)(2,1)}, f32[1,14,16]{2,1,0:T(8,128)S(1)}) %merge.1, (bf16[1,1792,2048]{2,1,0:T(8,128)(2,1)}, f32[1,14,16]{2,1,0:T(8,128)S(1)}) %merge.1, ...), branch_computations={%region_3.4_spmd, %region_4.5_spmd, %region_5.6_spmd, %region_6.7_... | conditional | bytes 16 | solution.py:428
  42.7 123.2 %spread.103 = (bf16[4,224,2048]{2,1,0:T(8,128)(2,1)}, f32[8,14,16]{2,1,0:T(8,128)S(1)}, bf16[3,224,2048]{2,1,0:T(8,128)(2,1)}) custom-call(bf16[1,1792,2048]{2,1,0:T(8,128)(2,1)} %get-tuple-element.412.quant, f32[1,14,16]{2,1,0:T(8,128)S(1)} %get-tuple-element.413.scale), custom_call_target="tpu_custom_call" | custom-call | tf_op jit(solution)/shard_map/cond/branch_33_fun/spread/pallas_call | solution.py:348
  166.2 0.0 copy-done
  166.2 0.7 convert_reduce_fusion.where
  166.9 7.0 %place.1 = (bf16[4,224,2048]{2,1,0:T(8,128)(2,1)}, f32[4,14,16]{2,1,0:T(8,128)}) custom-call(s32[4]{0:T(128)} %convert_reduce_fusion.where, s32[4]{0:T(128)} %plan.1, bf16[4,224,2048]{2,1,0:T(8,128)(2,1)} %get-tuple-element.576.held, f32[8,14,16]{2,1,0:T(8,128)S(1)} %get-tuple-element.577.scales), custom_call_target="tpu_custom_call" | custom-call | tf_op jit(solution)/shard_map/place/pallas_call | solution.py:386
  173.9 1.4 copy.17
  175.3 0.6 copy.16
Async XLA Ops:
  42.7 123.4 %copy-start = (s32[4]{0:T(128)S(1)}, s32[4]{0:T(128)}, u32[]{:S(2)}) copy-start(s32[4]{0:T(128)} %plan.1) | copy-start | bytes 52
